TPU v7x, 32 devices: a whole 2x2x4 slice. The times are simulated.
32 devices in a mesh: req: 4 (over y, core), seq: 8 (over z, x).
Axes of the slice: x: 2, y: 2, z: 4, core: 2. Of those that a mesh axis runs over, the one named last changes fastest.
Arguments:
- embedded: bfloat16 [4, 48, 3584], P(None, 'req'), may hold values from -6 to 6
- cache_keys: bfloat16 [4, 4096, 2048], P('req', 'seq'), may hold values from -6 to 6
- cache_values: bfloat16 [4, 4096, 2048], P('req', 'seq'), may hold values from -6 to 6
- token_owner: int32 [4, 4096], P('req', 'seq'), may hold values from 0 to 11, as said below
- dealing: int32 [48], replicated, may hold values from 0 to 47, as said below
- lengths: int32 [48], replicated, may hold values from 1 to 2048, as said below
- project_weight: bfloat16 [3584, 8192], P(None, 'seq')
- output_weight: bfloat16 [4096, 3584], P('seq'), may hold values from -0.09375 to 0.09375
- gate_weight: bfloat16 [3584, 14336], P(None, ('req', 'seq')), may hold values from -0.09375 to 0.09375
- up_weight: bfloat16 [3584, 14336], P(None, ('req', 'seq')), may hold values from -0.09375 to 0.09375
- down_weight: bfloat16 [14336, 3584], P(('req', 'seq')), may hold values from -0.046875 to 0.046875
- gain_first: float32 [3584], replicated, may hold values from 0.1 to 1.9
- gain_second: float32 [3584], replicated, may hold values from 0.1 to 1.9
- gain_third: float32 [3584], replicated, may hold values from 0.1 to 1.9
- gain_fourth: float32 [3584], replicated, may hold values from 0.1 to 1.9
Outputs:
- results: bfloat16 [4, 48, 3584], P(None, 'req')
Inputs may be any that keep to these rules, and one draw needn't show every extreme that they name: A permutation of the requests; slot i of req group g serves request dealing[g * 12 + i]. The lengths of the 12 requests dealt to one group sum to 4096; in every group the longest is exactly 2048. `token_owner`: each slot owns a contiguous run of its group's pool, runs in slot order, as many tokens as its request's length.
All inputs are finite; a program needn't handle non-finite values.
Results may differ from a plain program's by a relative error of at most 0.012.
The roundings to bfloat16 on the way count: a program that leaves them out, or rounds other values in their place, can miss the bound.
Values may be sent and summed in bfloat16 or wider, within the bound.
A program may use at most 128 MiB of HBM per device.

v0:
```python
import math
import jax
import jax.numpy as jnp
from jax import lax
from jax.sharding import PartitionSpec as P

H = 16
KVH = 8
HD = 256
STEPS = 4
soft_cap = 50.0
epsilon = 1e-06


def rms_scale(values, gain):
    mean_square = jnp.mean(values * values, axis=-1, keepdims=True)
    return values * lax.rsqrt(mean_square + epsilon) * gain


def rotate(values, positions):
    half_width = values.shape[-1] // 2
    freq_index = jnp.arange(half_width, dtype=jnp.float32)
    inverse = jnp.exp(freq_index * (-2.0 * math.log(10000.0) / values.shape[-1]))
    angles = positions[:, None] * inverse[None, :]
    cosine = jnp.cos(angles)[:, None, :]
    sine = jnp.sin(angles)[:, None, :]
    first_half = values[..., :half_width]
    second_half = values[..., half_width:]
    return jnp.concatenate(
        [first_half * cosine - second_half * sine, second_half * cosine + first_half * sine],
        axis=-1,
    )


def capped_weight(scores):
    return jnp.exp(soft_cap * jnp.tanh(scores / soft_cap))


def rounded(values):
    return lax.optimization_barrier(values.astype(jnp.bfloat16)).astype(jnp.float32)


def body(
    embedded,
    cache_keys,
    cache_values,
    token_owner,
    dealing,
    lengths,
    project_weight,
    output_weight,
    gate_weight,
    up_weight,
    down_weight,
    gain_first,
    gain_second,
    gain_third,
    gain_fourth,
):
    row_count = embedded.shape[1]
    rows = STEPS * row_count
    width = embedded.shape[2]
    local_tokens = cache_keys.shape[1]
    value_width = cache_keys.shape[2]
    group_size = H // KVH
    attention_width = H * HD
    column_count = output_weight.shape[0]
    group_index = lax.axis_index("req")
    seq_index = lax.axis_index("seq")
    seq_size = lax.axis_size("seq")
    req_size = lax.axis_size("req")
    column_start = seq_index * column_count
    slot_requests = lax.dynamic_slice_in_dim(dealing, group_index * row_count, row_count)
    matches = slot_requests[:, None] == jnp.arange(dealing.shape[0], dtype=jnp.int32)[None, :]
    base_positions = jnp.sum(jnp.where(matches, lengths[None, :], 0), axis=1)
    positions = base_positions[None, :] + jnp.arange(STEPS, dtype=jnp.int32)[:, None]
    positions = positions.reshape(rows).astype(jnp.float32)
    key_pool = cache_keys[0].reshape(local_tokens, KVH, HD)
    value_pool = cache_values[0].reshape(local_tokens, KVH, HD)
    slots = jnp.tile(jnp.arange(row_count, dtype=jnp.int32), STEPS)
    moments = jnp.repeat(jnp.arange(STEPS, dtype=jnp.int32), row_count)
    owned_mask = token_owner[0][None, :] == slots[:, None]
    stream = embedded.reshape(rows, width).astype(jnp.float32)
    normed = rms_scale(stream, gain_first).astype(jnp.bfloat16)
    local_part = jnp.dot(normed, project_weight, preferred_element_type=jnp.float32).astype(
        jnp.bfloat16
    )
    projected = lax.all_gather(local_part, "seq", axis=1, tiled=True)
    query_rows = projected[:, :attention_width].astype(jnp.float32).reshape(rows, H, HD)
    queries = (rotate(query_rows, positions) * HD ** (-0.5)).astype(jnp.bfloat16)
    key_rows = (
        projected[:, attention_width : attention_width + value_width]
        .astype(jnp.float32)
        .reshape(rows, KVH, HD)
    )
    fresh_keys = rotate(key_rows, positions).astype(jnp.bfloat16)
    fresh_values = projected[:, attention_width + value_width :].reshape(rows, KVH, HD)
    grouped = queries.reshape(rows, KVH, group_size, HD)
    all_keys = jnp.concatenate([key_pool, fresh_keys], axis=0)
    all_values = jnp.concatenate([value_pool, fresh_values], axis=0)
    fresh_mask = (
        (slots[None, :] == slots[:, None])
        & (moments[None, :] <= moments[:, None])
        & (seq_index == 0)
    )
    mask = jnp.concatenate([owned_mask, fresh_mask], axis=1)
    scores = jnp.einsum("igqd,tgd->igqt", grouped, all_keys, preferred_element_type=jnp.float32)
    weights = jnp.where(mask[:, None, None, :], capped_weight(scores), 0.0)
    totals = lax.psum(jnp.sum(weights, axis=-1), "seq").reshape(rows, H)
    outputs = jnp.einsum(
        "igqt,tgd->igqd",
        weights.astype(jnp.bfloat16),
        all_values,
        preferred_element_type=jnp.float32,
    ).reshape(rows, attention_width)
    outputs = lax.psum_scatter(outputs, "seq", scatter_dimension=1, tiled=True)
    spread = jnp.repeat(totals, HD, axis=1)
    spread = lax.dynamic_slice_in_dim(spread, column_start, column_count, 1)
    attended = (outputs / spread).astype(jnp.bfloat16)
    partial = jnp.dot(attended, output_weight, preferred_element_type=jnp.float32)
    mixed = lax.psum(partial, "seq")
    middle = stream + rms_scale(mixed, gain_second)
    feed_input = rms_scale(middle, gain_third).astype(jnp.bfloat16)
    block_rows = lax.all_gather(feed_input, "req", axis=0, tiled=True)
    gate_part = jnp.dot(block_rows, gate_weight, preferred_element_type=jnp.float32)
    up_part = jnp.dot(block_rows, up_weight, preferred_element_type=jnp.float32)
    hidden = (jax.nn.gelu(gate_part, approximate=True) * up_part).astype(jnp.bfloat16)
    summed = jnp.dot(hidden, down_weight, preferred_element_type=jnp.float32)
    summed = lax.psum_scatter(summed, "req", scatter_dimension=0, tiled=True)
    summed = lax.psum(summed, "seq")
    results = (middle + rms_scale(summed, gain_fourth)).astype(jnp.bfloat16)
    return results.reshape(STEPS, row_count, width)


def solution(mesh):
    return jax.shard_map(
        body,
        mesh=mesh,
        in_specs=(
            P(None, "req", None),
            P("req", "seq", None),
            P("req", "seq", None),
            P("req", "seq"),
            P(),
            P(),
            P(None, "seq"),
            P("seq", None),
            P(None, ("req", "seq")),
            P(None, ("req", "seq")),
            P(("req", "seq"), None),
            P(),
            P(),
            P(),
            P(),
        ),
        out_specs=P(None, "req", None),
        check_vma=False,
    )
```

profile of v0, /device:TPU:0, one launch (start us, length us, event | category | flops | bytes accessed | tf_op | source)
XLA Modules:
  0.0 383.3 jit_solution(17114336762805842567)
XLA Ops:
  6.6 2.1 copy.64
  8.7 1.2 multiply_reduce_fusion.3
  9.9 2.1 reshape.160
  12.1 0.1 copy.86
  12.2 0.1 rsqrt.36
  12.2 4.8 %convolution_convert_fusion = bf16[48,1024]{1,0:T(8,128)(2,1)S(1)} fusion(bf16[3584,1024]{1,0:T(8,128)(2,1)} %param.21, f32[48,3584]{1,0:T(8,128)} %reshape.160, f32[3584]{0:T(1024)S(1)} %copy-done.4, f32[48]{0:T(128)S(1)} %rsqrt.36), kind=kOutput, calls=%fused_computation.14 | convolution fusion | flops 352886784 | bytes 8140992 | tf_op jit(solution)/shard_map/dot_general | solution.py:85
  17.0 0.0 copy-start.8
  17.0 0.0 copy-start.9
  17.0 33.8 %all_gather.6 = bf16[48,8192]{1,0:T(8,128)(2,1)S(1)} all-gather(bf16[48,1024]{1,0:T(8,128)(2,1)S(1)} %convolution_convert_fusion), channel_id=1, replica_groups=mesh['req'=4,'seq'=8] {'seq'}, dimensions={1}, use_global_device_ids=true | all-gather | bytes 884736 | tf_op jit(solution)/shard_map/all_gather | solution.py:88
  50.9 0.9 slice_convert_fusion.1
  51.7 0.9 slice_convert_fusion
  52.6 0.1 dynamic_slice.6
  52.7 0.2 select_reduce_fusion
  52.9 0.1 add.91
  53.0 0.1 le.17
  53.1 1.1 copy.83
  54.2 0.7 fusion.39
  54.9 1.4 copy.84
  56.3 0.2 multiply_cosine_fusion
  56.5 0.1 multiply_subtract_fusion
  56.6 0.9 copy.73
  57.5 0.9 copy.74
  58.3 0.1 eq.50
  58.4 0.1 and_and_fusion
  58.5 0.1 broadcast_compare_fusion
  58.6 3.9 %copy.69 = bf16[1,512,2048]{1,2,0:T(8,128)(2,1)} copy(bf16[1,512,2048]{2,1,0:T(8,128)(2,1)} %param.16) | data formatting | bytes 4194304 | tf_op args[1]
  62.6 3.9 %copy.72 = bf16[512,8,256]{2,0,1:T(8,128)(2,1)} copy(bf16[512,8,256]{0,2,1:T(8,128)(2,1)} %bitcast.44) | data formatting | bytes 4194304 | tf_op jit(solution)/shard_map/reshape;squeeze | solution.py:78
  66.5 1.6 copy.92
  68.1 3.9 %copy.65 = bf16[1,512,2048]{1,2,0:T(8,128)(2,1)} copy(bf16[1,512,2048]{2,1,0:T(8,128)(2,1)} %param.17) | data formatting | bytes 4194304 | tf_op args[2]
  72.0 3.9 %copy.67 = bf16[512,8,256]{2,0,1:T(8,128)(2,1)} copy(bf16[512,8,256]{0,2,1:T(8,128)(2,1)} %bitcast.45) | data formatting | bytes 4194304 | tf_op jit(solution)/shard_map/reshape;squeeze | solution.py:79
  76.0 1.0 subtract_convert_fusion
  77.0 2.9 fusion.40
  80.0 0.6 fusion.8
  80.5 1.5 copy.75
  82.1 2.6 reshape.156
  84.7 0.0 reduce-scatter.3.cloned.1.call-update
  84.7 0.0 all-reduce.3.cloned.1.call-start
  84.8 21.7 %psum.21 = f32[48,16]{0,1:T(8,128)S(1)} all-reduce(f32[48,16]{0,1:T(8,128)S(1)} %bitcast.56), channel_id=1, replica_groups=mesh['req'=4,'seq'=8] {'seq'}, use_global_device_ids=true, to_apply=%region_4.5 | all-reduce | flops 768 | bytes 6144 | tf_op jit(solution)/shard_map/psum | solution.py:109
  106.4 0.1 copy.76
  106.5 0.2 broadcast_in_dim.35
  106.7 1.4 copy.85
  108.1 40.9 %reduce-scatter.3.cloned.1.call-done = f32[48,512]{1,0:T(8,128)} async-done(((f32[48,4096]{1,0:T(8,128)}), f32[48,512]{1,0:T(8,128)}) %reduce-scatter.3.cloned.1.call-update) | async-done | bytes 98320 | tf_op jit(solution)/shard_map/reduce_scatter | solution.py:116
  149.0 3.8 fusion.29
  152.7 0.0 all-reduce.3.cloned.1.call-update
  152.7 0.0 all-gather.2.cloned.1.call-start
  152.8 72.8 %all-reduce.3.cloned.1.call-done = f32[48,3584]{1,0:T(8,128)} async-done(((f32[48,3584]{1,0:T(8,128)}), f32[48,3584]{1,0:T(8,128)}) %all-reduce.3.cloned.1.call-update) | async-done | bytes 688144 | tf_op jit(solution)/shard_map/psum | solution.py:121
  225.6 1.2 multiply_reduce_fusion.2
  226.9 1.6 multiply_reduce_fusion.1
  228.5 0.8 copy-done.1
  229.3 0.9 multiply_convert_fusion
  230.2 0.0 all-gather.2.cloned.1.call-update
  230.2 0.0 reduce-scatter.5.cloned.1.call-start
  230.3 17.7 %all-gather.2.cloned.1.call-done = bf16[192,3584]{1,0:T(8,128)(2,1)} async-done(((bf16[48,3584]{1,0:T(8,128)(2,1)}), bf16[192,3584]{1,0:T(8,128)(2,1)}) %all-gather.2.cloned.1.call-update) | async-done | bytes 1376272 | tf_op jit(solution)/shard_map/all_gather | solution.py:124
  247.9 4.1 %fusion.41 = f32[192,448]{1,0:T(8,128)} fusion(bf16[192,3584]{1,0:T(8,128)(2,1)} %all-gather.2.cloned.1.call-done, bf16[3584,448]{0,1:T(8,128)(2,1)} %param.23), kind=kOutput, calls=%fused_computation.75 | convolution fusion | flops 616562688 | bytes 4931584 | tf_op jit(solution)/shard_map/dot_general | solution.py:125
  252.1 6.0 %fusion.10 = f32[192,3584]{1,0:T(8,128)} fusion(bf16[448,3584]{1,0:T(8,128)(2,1)S(1)} %copy-done, bf16[192,3584]{1,0:T(8,128)(2,1)} %all-gather.2.cloned.1.call-done, bf16[3584,448]{0,1:T(8,128)(2,1)} %param.24, f32[192,448]{1,0:T(8,128)} %fusion.41), kind=kOutput, calls=%fused_computation.15 | convolution fusion | flops 1233985536 | bytes 10895360 | tf_op jit(solution)/shard_map/dot_general | solution.py:128
  258.1 0.0 reduce-scatter.5.cloned.1.call-update
  258.1 0.0 all-reduce.5.cloned.1.call-start
  258.2 35.6 %reduce-scatter.5.cloned.1.call-done = f32[48,3584]{1,0:T(8,128)} async-done(((f32[192,3584]{1,0:T(8,128)}), f32[48,3584]{1,0:T(8,128)}) %reduce-scatter.5.cloned.1.call-update) | async-done | bytes 688144 | tf_op jit(solution)/shard_map/reduce_scatter | solution.py:129
  293.7 0.0 all-reduce.5.cloned.1.call-update
  293.8 77.4 %all-reduce.5.cloned.1.call-done = f32[48,3584]{1,0:T(8,128)} async-done(((f32[48,3584]{1,0:T(8,128)}), f32[48,3584]{1,0:T(8,128)}) %all-reduce.5.cloned.1.call-update) | async-done | bytes 688144 | tf_op jit(solution)/shard_map/psum | solution.py:130
  371.1 1.2 multiply_reduce_fusion
  372.4 1.5 add_convert_fusion
  373.9 0.9 reshape.159
  374.7 2.0 copy.77
  (28 shorter events, 0.1 us)
Async XLA Ops:
  6.5 245.5 %copy-start = (bf16[448,3584]{1,0:T(8,128)(2,1)S(1)}, bf16[448,3584]{1,0:T(8,128)(2,1)}, u32[]{:S(2)}) copy-start(bf16[448,3584]{1,0:T(8,128)(2,1)} %param.25) | copy-start | bytes 9633796
  6.5 5.7 %copy-start.4 = (f32[3584]{0:T(1024)S(1)}, f32[3584]{0:T(1024)}, u32[]{:S(2)}) copy-start(f32[3584]{0:T(1024)} %param.26) | copy-start | bytes 43012
  6.5 142.4 %reduce-scatter.3.cloned.1.call-start = ((), (), s32[]{:S(2)}) async-start(), calls=%async_computation.2 | async-start | bytes 884736 | tf_op jit(solution)/shard_map/reduce_scatter | solution.py:116
  17.0 35.6 %copy-start.8 = (s32[48]{0:T(128)S(1)}, s32[48]{0:T(128)}, u32[]{:S(2)}) copy-start(s32[48]{0:T(128)} %param.19) | copy-start | bytes 580
  17.0 35.7 %copy-start.9 = (s32[48]{0:T(128)S(1)}, s32[48]{0:T(128)}, u32[]{:S(2)}) copy-start(s32[48]{0:T(128)} %param.20) | copy-start | bytes 580
  54.9 3.6 copy-start.7
  77.0 2.9 copy-start.2
  77.0 2.9 copy-start.3
  84.7 140.9 %all-reduce.3.cloned.1.call-start = ((), (), s32[]{:S(2)}) async-start(), calls=%async_computation.3 | async-start | bytes 1376256 | tf_op jit(solution)/shard_map/psum | solution.py:121
  149.0 77.9 %copy-start.6 = (f32[3584]{0:T(1024)S(1)}, f32[3584]{0:T(1024)}, u32[]{:S(2)}) copy-start(f32[3584]{0:T(1024)} %param.27) | copy-start | bytes 43012
  152.7 76.6 %copy-start.5 = (f32[3584]{0:T(1024)S(1)}, f32[3584]{0:T(1024)}, u32[]{:S(2)}) copy-start(f32[3584]{0:T(1024)} %param.28) | copy-start | bytes 43012
  152.7 95.2 %all-gather.2.cloned.1.call-start = ((), (), s32[]{:S(2)}) async-start(), calls=%async_computation.4 | async-start | bytes 1720320 | tf_op jit(solution)/shard_map/all_gather | solution.py:124
  228.4 0.9 copy-start.1
  230.2 63.5 %reduce-scatter.5.cloned.1.call-start = ((), (), s32[]{:S(2)}) async-start(), calls=%async_computation.5 | async-start | bytes 3440640 | tf_op jit(solution)/shard_map/reduce_scatter | solution.py:129
  258.1 113.0 %all-reduce.5.cloned.1.call-start = ((), (), s32[]{:S(2)}) async-start(), calls=%async_computation.6 | async-start | bytes 1376256 | tf_op jit(solution)/shard_map/psum | solution.py:130
Sparse Core Ops, SparseCore 0:
  84.8 64.0 reduce-scatter.2
  152.9 72.6 all-reduce.2
  230.3 17.5 all-gather.1
  258.2 35.4 reduce-scatter.4
  297.4 73.6 all-reduce.4
where the time goes:
time: 384 us; the launch traced here: 383 us
  waiting for transfers between devices  244 us (64%)
  blocking collectives  55.5 us (14%)
  local copies, waits for them, and re-layouts  36.6 us (10%)
  matrix products  22.2 us (6%)
  between operations  13.3 us (3%)
  other arithmetic  11.1 us (3%)
    psum x1, waiting for transfers between devices, body(): summed = lax.psum(summed, 'seq')  77.4 us
    psum x1, waiting for transfers between devices, body(): mixed = lax.psum(partial, 'seq')  72.8 us
    reduce_scatter x1, waiting for transfers between devices, body(): outputs = lax.psum_scatter(outputs, 'seq', scatter_dimension=1, tiled=True)  40.9 us
    reduce_scatter x1, waiting for transfers between devices, body(): summed = lax.psum_scatter(summed, 'req', scatter_dimension=0, tiled=True)  35.6 us
    all_gather x1, blocking collectives, body(): projected = lax.all_gather(local_part, 'seq', axis=1, tiled=True)  33.8 us
    psum x1, blocking collectives, body(): totals = lax.psum(jnp.sum(weights, axis=-1), 'seq').reshape(rows, H)  21.7 us
    all_gather x1, waiting for transfers between devices, body(): block_rows = lax.all_gather(feed_input, 'req', axis=0, tiled=True)  17.7 us
    unnamed x26, local copies, waits for them, and re-layouts  12.7 us
  transfers between devices with their start and end apart: 5, of which 5 were waited for; matrix products, arithmetic and copies ran while one was open for 0% of the time, Pallas kernels for 0%

commit v1 on v0

--- a/solution.py
+++ b/solution.py
@@ -1,3 +1,4 @@
+import functools
 import math
 import jax
 import jax.numpy as jnp
@@ -10,6 +11,14 @@
 STEPS = 4
 soft_cap = 50.0
 epsilon = 1e-06
+
+
+def update_view(x_part, row_axis):
+    tall = lax.all_gather(x_part, axis_name=row_axis)
+    return jnp.sum(tall, axis=0)
+
+
+review_the_heaps = functools.partial(update_view, row_axis="seq")
 
 
 def rms_scale(values, gain):
@@ -127,7 +136,7 @@
     hidden = (jax.nn.gelu(gate_part, approximate=True) * up_part).astype(jnp.bfloat16)
     summed = jnp.dot(hidden, down_weight, preferred_element_type=jnp.float32)
     summed = lax.psum_scatter(summed, "req", scatter_dimension=0, tiled=True)
-    summed = lax.psum(summed, "seq")
+    summed = review_the_heaps(summed)
     results = (middle + rms_scale(summed, gain_fourth)).astype(jnp.bfloat16)
     return results.reshape(STEPS, row_count, width)
 

time: 384 us -> 401 us (1.044)
  waiting for transfers between devices: 244 us -> 259 us
    all_gather x0 -> x1, waiting for transfers between devices: none -> 91.7 us  [update_view(): tall = lax.all_gather(x_part, axis_name=row_axis)]
    psum x1 -> x0, waiting for transfers between devices: 77.4 us -> none  [body(): summed = lax.psum(summed, 'seq')]
where the time goes in v1:
time: 401 us
  waiting for transfers between devices  259 us (65%)
  blocking collectives  55.6 us (14%)
  local copies, waits for them, and re-layouts  35.5 us (9%)
  matrix products  22.1 us (6%)
  other arithmetic  15 us (4%)
  between operations  13.3 us (3%)
    all_gather x1, waiting for transfers between devices, update_view(): tall = lax.all_gather(x_part, axis_name=row_axis)  91.7 us
    psum x1, waiting for transfers between devices, body(): mixed = lax.psum(partial, 'seq')  72.8 us
    reduce_scatter x1, waiting for transfers between devices, body(): outputs = lax.psum_scatter(outputs, 'seq', scatter_dimension=1, tiled=True)  40.9 us
    reduce_scatter x1, waiting for transfers between devices, body(): summed = lax.psum_scatter(summed, 'req', scatter_dimension=0, tiled=True)  35.6 us
    all_gather x1, blocking collectives, body(): projected = lax.all_gather(local_part, 'seq', axis=1, tiled=True)  33.9 us
    psum x1, blocking collectives, body(): totals = lax.psum(jnp.sum(weights, axis=-1), 'seq').reshape(rows, H)  21.7 us
    all_gather x1, waiting for transfers between devices, body(): block_rows = lax.all_gather(feed_input, 'req', axis=0, tiled=True)  17.7 us
    unnamed x26, local copies, waits for them, and re-layouts  12.7 us
  transfers between devices with their start and end apart: 5, of which 5 were waited for; matrix products, arithmetic and copies ran while one was open for 0% of the time, Pallas kernels for 0%

profile of v1, /device:TPU:0, one launch (start us, length us, event | category | flops | bytes accessed | tf_op | source)
XLA Modules:
  0.0 400.5 jit_solution(16415823163129064840)
XLA Ops:
  6.6 1.4 multiply_reduce_fusion.3
  7.9 2.0 copy.64
  9.9 0.1 copy.86
  10.0 0.1 rsqrt.36
  10.1 2.1 reshape.160
  12.3 4.8 %convolution_convert_fusion = bf16[48,1024]{1,0:T(8,128)(2,1)S(1)} fusion(bf16[3584,1024]{1,0:T(8,128)(2,1)} %param.21, f32[48,3584]{1,0:T(8,128)} %reshape.160, f32[3584]{0:T(1024)S(1)} %copy-done.4, f32[48]{0:T(128)S(1)} %rsqrt.36), kind=kOutput, calls=%fused_computation.14 | convolution fusion | flops 352886784 | bytes 8140992 | tf_op jit(solution)/shard_map/dot_general | solution.py:94
  17.0 0.0 copy-start.7
  17.1 33.9 %all_gather.12 = bf16[48,8192]{1,0:T(8,128)(2,1)S(1)} all-gather(bf16[48,1024]{1,0:T(8,128)(2,1)S(1)} %convolution_convert_fusion), channel_id=1, replica_groups=mesh['req'=4,'seq'=8] {'seq'}, dimensions={1}, use_global_device_ids=true | all-gather | bytes 884736 | tf_op jit(solution)/shard_map/all_gather | solution.py:97
  51.0 0.8 slice_convert_fusion.1
  51.8 0.9 slice_convert_fusion
  52.7 0.1 dynamic_slice.6
  52.8 0.2 select_reduce_fusion
  53.0 0.1 add.89
  53.1 0.1 le.17
  53.2 0.1 eq.50
  53.3 0.1 and_and_fusion
  53.4 0.1 broadcast_compare_fusion
  53.5 1.4 copy.84
  54.8 1.1 copy.83
  56.0 0.7 copy.92
  56.6 0.7 fusion.39
  57.3 0.2 multiply_cosine_fusion
  57.5 0.1 multiply_subtract_fusion
  57.6 0.9 copy.73
  58.5 0.9 copy.74
  59.4 3.9 copy.69
  63.3 3.9 copy.72
  67.2 3.9 copy.65
  71.2 3.9 copy.67
  75.1 1.0 subtract_convert_fusion
  76.1 2.9 fusion.40
  79.1 0.6 fusion.8
  79.7 1.5 copy.75
  81.2 2.6 reshape.156
  83.8 0.0 reduce-scatter.3.cloned.1.call-update
  83.8 0.0 all-reduce.2.cloned.1.call-start
  83.9 21.7 %psum.14 = f32[48,16]{0,1:T(8,128)S(1)} all-reduce(f32[48,16]{0,1:T(8,128)S(1)} %bitcast.58), channel_id=1, replica_groups=mesh['req'=4,'seq'=8] {'seq'}, use_global_device_ids=true, to_apply=%region_4.5 | all-reduce | flops 768 | bytes 6144 | tf_op jit(solution)/shard_map/psum | solution.py:118
  105.6 0.1 copy.76
  105.7 0.2 broadcast_in_dim.35
  105.8 1.4 copy.85
  107.2 40.9 %reduce-scatter.3.cloned.1.call-done = f32[48,512]{1,0:T(8,128)} async-done(((f32[48,4096]{1,0:T(8,128)}), f32[48,512]{1,0:T(8,128)}) %reduce-scatter.3.cloned.1.call-update) | async-done | bytes 98320 | tf_op jit(solution)/shard_map/reduce_scatter | solution.py:125
  148.1 3.8 fusion.29
  151.9 0.0 all-reduce.2.cloned.1.call-update
  151.9 0.0 all-gather.4.cloned.1.call-start
  152.0 72.8 %all-reduce.2.cloned.1.call-done = f32[48,3584]{1,0:T(8,128)} async-done(((f32[48,3584]{1,0:T(8,128)}), f32[48,3584]{1,0:T(8,128)}) %all-reduce.2.cloned.1.call-update) | async-done | bytes 688144 | tf_op jit(solution)/shard_map/psum | solution.py:130
  224.8 1.2 multiply_reduce_fusion.2
  226.0 1.6 multiply_reduce_fusion.1
  227.7 0.9 copy-done.1
  228.5 0.9 multiply_convert_fusion
  229.4 0.0 all-gather.4.cloned.1.call-update
  229.4 0.0 reduce-scatter.5.cloned.1.call-start
  229.5 17.7 %all-gather.4.cloned.1.call-done = bf16[192,3584]{1,0:T(8,128)(2,1)} async-done(((bf16[48,3584]{1,0:T(8,128)(2,1)}), bf16[192,3584]{1,0:T(8,128)(2,1)}) %all-gather.4.cloned.1.call-update) | async-done | bytes 1376272 | tf_op jit(solution)/shard_map/all_gather | solution.py:133
  247.1 4.1 %fusion.41 = f32[192,448]{1,0:T(8,128)} fusion(bf16[192,3584]{1,0:T(8,128)(2,1)} %all-gather.4.cloned.1.call-done, bf16[3584,448]{0,1:T(8,128)(2,1)} %param.23), kind=kOutput, calls=%fused_computation.75 | convolution fusion | flops 616562688 | bytes 4931584 | tf_op jit(solution)/shard_map/dot_general | solution.py:134
  251.3 6.0 %fusion.10 = f32[192,3584]{1,0:T(8,128)} fusion(bf16[448,3584]{1,0:T(8,128)(2,1)S(1)} %copy-done, bf16[192,3584]{1,0:T(8,128)(2,1)} %all-gather.4.cloned.1.call-done, bf16[3584,448]{0,1:T(8,128)(2,1)} %param.24, f32[192,448]{1,0:T(8,128)} %fusion.41), kind=kOutput, calls=%fused_computation.15 | convolution fusion | flops 1233985536 | bytes 10895360 | tf_op jit(solution)/shard_map/dot_general | solution.py:137
  257.3 0.0 reduce-scatter.5.cloned.1.call-update
  257.3 0.0 all-gather.6.cloned.1.call-start
  257.3 35.6 %reduce-scatter.5.cloned.1.call-done = f32[48,3584]{1,0:T(8,128)} async-done(((f32[192,3584]{1,0:T(8,128)}), f32[48,3584]{1,0:T(8,128)}) %reduce-scatter.5.cloned.1.call-update) | async-done | bytes 688144 | tf_op jit(solution)/shard_map/reduce_scatter | solution.py:138
  292.9 0.0 all-gather.6.cloned.1.call-update
  292.9 91.7 %all-gather.6.cloned.1.call-done = f32[384,3584]{1,0:T(8,128)} async-done(((f32[48,3584]{1,0:T(8,128)}), f32[384,3584]{1,0:T(8,128)}) %all-gather.6.cloned.1.call-update) | async-done | bytes 5505040 | tf_op jit(solution)/shard_map/all_gather | solution.py:17
  384.7 3.7 reduce_sum.68
  388.4 1.2 multiply_reduce_fusion
  389.7 1.5 add_convert_fusion
  391.1 0.9 reshape.159
  392.0 2.0 copy.77
  (29 shorter events, 0.1 us)
Async XLA Ops:
  6.5 244.7 %copy-start = (bf16[448,3584]{1,0:T(8,128)(2,1)S(1)}, bf16[448,3584]{1,0:T(8,128)(2,1)}, u32[]{:S(2)}) copy-start(bf16[448,3584]{1,0:T(8,128)(2,1)} %param.25) | copy-start | bytes 9633796
  6.5 5.7 %copy-start.4 = (f32[3584]{0:T(1024)S(1)}, f32[3584]{0:T(1024)}, u32[]{:S(2)}) copy-start(f32[3584]{0:T(1024)} %param.26) | copy-start | bytes 43012
  6.5 141.6 %reduce-scatter.3.cloned.1.call-start = ((), (), s32[]{:S(2)}) async-start(), calls=%async_computation.2 | async-start | bytes 884736 | tf_op jit(solution)/shard_map/reduce_scatter | solution.py:125
  17.0 35.7 %copy-start.8 = (s32[48]{0:T(128)S(1)}, s32[48]{0:T(128)}, u32[]{:S(2)}) copy-start(s32[48]{0:T(128)} %param.19) | copy-start | bytes 580
  17.0 35.8 %copy-start.9 = (s32[48]{0:T(128)S(1)}, s32[48]{0:T(128)}, u32[]{:S(2)}) copy-start(s32[48]{0:T(128)} %param.20) | copy-start | bytes 580
  17.0 36.3 %copy-start.7 = (s32[1,512]{1,0:T(1,128)S(1)}, s32[1,512]{1,0:T(1,128)}, u32[]{:S(2)}) copy-start(s32[1,512]{1,0:T(1,128)} %param.18) | copy-start | bytes 6148
  76.1 2.9 copy-start.2
  76.1 2.9 copy-start.3
  83.8 140.9 %all-reduce.2.cloned.1.call-start = ((), (), s32[]{:S(2)}) async-start(), calls=%async_computation.3 | async-start | bytes 1376256 | tf_op jit(solution)/shard_map/psum | solution.py:130
  148.1 77.9 %copy-start.6 = (f32[3584]{0:T(1024)S(1)}, f32[3584]{0:T(1024)}, u32[]{:S(2)}) copy-start(f32[3584]{0:T(1024)} %param.27) | copy-start | bytes 43012
  151.9 76.6 %copy-start.5 = (f32[3584]{0:T(1024)S(1)}, f32[3584]{0:T(1024)}, u32[]{:S(2)}) copy-start(f32[3584]{0:T(1024)} %param.28) | copy-start | bytes 43012
  151.9 95.2 %all-gather.4.cloned.1.call-start = ((), (), s32[]{:S(2)}) async-start(), calls=%async_computation.4 | async-start | bytes 1720320 | tf_op jit(solution)/shard_map/all_gather | solution.py:133
  227.6 0.9 copy-start.1
  229.4 63.5 %reduce-scatter.5.cloned.1.call-start = ((), (), s32[]{:S(2)}) async-start(), calls=%async_computation.5 | async-start | bytes 3440640 | tf_op jit(solution)/shard_map/reduce_scatter | solution.py:138
  257.3 127.4 %all-gather.6.cloned.1.call-start = ((), (), s32[]{:S(2)}) async-start(), calls=%async_computation.6 | async-start | bytes 6193152 | tf_op jit(solution)/shard_map/all_gather | solution.py:17
Sparse Core Ops, SparseCore 0:
  84.0 64.1 reduce-scatter.2
  152.0 72.6 all-reduce.1
  229.5 17.5 all-gather.3
  257.4 35.4 reduce-scatter.4
  295.2 89.4 all-gather.5
